TPU v7x, 128 devices: a whole 4x4x4 slice. The times are simulated.
128 devices in a mesh: samp: 32 (over x, y, core), var: 4 (over z).
Axes of the slice: x: 4, y: 4, z: 4, core: 2. Of those that a mesh axis runs over, the one named last changes fastest.
Arguments:
- genotypes: int32 [32768, 4096], P('samp', 'var'), may hold values from 0 to 2
- observed: int32 [32768, 4096], P('samp', 'var'), may hold values from 0 to 1, as said below
- proportions: float32 [10, 32768], P(None, 'samp'), may hold values from 0 to 1, as said below
- frequencies: float32 [10, 4096], P(None, ('samp', 'var')), may hold values from 0.02 to 0.98
Outputs:
- mixture: float32 [10, 32768], P(None, 'samp')
- alleles: float32 [10, 4096], P(None, 'var')
Inputs may be any that keep to these rules, and one draw needn't show every extreme that they name: Every sample is observed at 256 or more variants and every variant at 2048 or more samples. Each sample's 10 proportions are positive and sum to one.
All inputs are finite; a program needn't handle non-finite values.
Results may differ from a plain program's by a relative error of at most 0.0003.
Values sent between devices are 32-bit elements; how exact they have to be, the bound alone decides.
A program may use at most 128 MiB of HBM per device.

v0:
```python
import jax
import jax.numpy as jnp
from jax import lax
from jax.sharding import PartitionSpec as P

STEPS = 2
CLIP_LOW = 1e-05
NORM_EPS = 1e-10
EXACT = lax.Precision.HIGHEST


def clip_unit(values):
    return jnp.clip(values, CLIP_LOW, 1.0 - CLIP_LOW)


def tidy_mixture(mixture):
    clipped = clip_unit(mixture)
    return clipped / jnp.sum(clipped, axis=0, keepdims=True)


def step_size(first, second):
    return jnp.maximum(1.0, jnp.sqrt(first / (second + NORM_EPS)))


def allele_rule(alleles, alt_sums, ref_sums):
    weighted = alleles * alt_sums
    return clip_unit(weighted / (weighted + (1.0 - alleles) * ref_sums))


def local(genotypes, observed, proportions, frequencies):
    var_count = lax.axis_size("var")
    gathered = lax.all_gather(frequencies, ("samp", "var"), axis=1, tiled=True)
    owner_width = gathered.shape[1] // var_count
    alleles = lax.dynamic_slice_in_dim(
        gathered, lax.axis_index("var") * owner_width, owner_width, 1
    )
    seen_vals = observed.astype(jnp.float32)
    geno_vals = genotypes.astype(jnp.float32)
    alt_counts = seen_vals * geno_vals
    ref_counts = seen_vals * (2.0 - geno_vals)
    local_counts = jnp.sum(observed, axis=1).astype(jnp.float32)
    twice_observed = 2.0 * lax.psum(local_counts, "var")[None, :]

    def expectation_step(mixture, current):
        expected = lax.dot_general(
            mixture,
            current,
            (((0,), (0,)), ((), ())),
            precision=EXACT,
            preferred_element_type=jnp.float32,
        )
        ratio_alt = alt_counts / expected
        ratio_ref = ref_counts / (1.0 - expected)
        prop_terms = lax.dot_general(
            current,
            ratio_alt - ratio_ref,
            (((1,), (1,)), ((), ())),
            precision=EXACT,
            preferred_element_type=jnp.float32,
        )
        prop_terms = prop_terms + jnp.sum(ratio_ref, axis=1)[None, :]
        alt_terms = lax.dot_general(
            mixture,
            ratio_alt,
            (((1,), (0,)), ((), ())),
            precision=EXACT,
            preferred_element_type=jnp.float32,
        )
        ref_terms = lax.dot_general(
            mixture,
            ratio_ref,
            (((1,), (0,)), ((), ())),
            precision=EXACT,
            preferred_element_type=jnp.float32,
        )
        prop_sums = lax.psum(prop_terms, "var")
        next_mixture = clip_unit(mixture * prop_sums / twice_observed)
        alt_sums, ref_sums = lax.psum((alt_terms, ref_terms), "samp")
        next_alleles = allele_rule(current, alt_sums, ref_sums)
        return (next_mixture, next_alleles)

    mixture = proportions
    for repeat in range(STEPS):
        mixture_one, alleles_one = expectation_step(mixture, alleles)
        mixture_two, alleles_two = expectation_step(mixture_one, alleles_one)
        step_mix = mixture_one - mixture
        curve_mix = mixture_two - mixture_one - step_mix
        step_allele = alleles_one - alleles
        curve_allele = alleles_two - alleles_one - step_allele
        step_mix_local = jnp.sum(step_mix * step_mix)
        curve_mix_local = jnp.sum(curve_mix * curve_mix)
        step_allele_local = jnp.sum(step_allele * step_allele)
        curve_allele_local = jnp.sum(curve_allele * curve_allele)
        step_allele_sum, curve_allele_sum = lax.psum((step_allele_local, curve_allele_local), "var")
        step_mix_sum, curve_mix_sum = lax.psum((step_mix_local, curve_mix_local), "samp")
        alpha_mix = step_size(step_mix_sum, curve_mix_sum)
        alpha_allele = step_size(step_allele_sum, curve_allele_sum)
        extra_mix = tidy_mixture(
            mixture + 2.0 * alpha_mix * step_mix + alpha_mix * alpha_mix * curve_mix
        )
        extra_allele = clip_unit(
            alleles + 2.0 * alpha_allele * step_allele + alpha_allele * alpha_allele * curve_allele
        )
        mixture, alleles = expectation_step(extra_mix, extra_allele)
    return (mixture, alleles)


def solution(mesh):
    placed = (P("samp", "var"), P("samp", "var"), P(None, "samp"), P(None, ("samp", "var")))
    return jax.shard_map(
        local,
        mesh=mesh,
        in_specs=placed,
        out_specs=(P(None, "samp"), P(None, "var")),
        check_vma=False,
    )
```

profile of v0, /device:TPU:1, one launch (start us, length us, event | category | flops | bytes accessed | tf_op | source)
XLA Modules:
  0.0 985.0 jit_solution(3233084332891088129)
XLA Ops:
  7.2 64.1 %all-gather = f32[128,32,10]{1,2,0:T(8,128)S(1)} all-gather(f32[1,32,10]{1,2,0:T(8,128)} %bitcast.70), channel_id=1, replica_groups=mesh['samp'=32,'var'=4] {'samp','var'}, dimensions={0}, use_global_device_ids=true | all-gather | bytes 165120 | tf_op jit(solution)/shard_map/all_gather | solution.py:32
  82.6 12.0 %fusion.78 = (f32[1024]{0:T(1024)S(1)}, f32[1024,1024]{0,1:T(8,128)S(1)}, f32[1024,1024]{0,1:T(8,128)}, f32[1024,1024]{0,1:T(8,128)S(1)}, f32[1024,1024]{1,0:T(8,128)S(1)}) fusion(s32[1024,1024]{0,1:T(8,128)} %copy.14, s32[1024,1024]{0,1:T(8,128)} %copy.13, f32[10,1024]{1,0:T(8,128)S(1)} %copy-done.11, f32[4096,10]{0,1:T(8,128)S(1)} %reshape.15, ...), kind=kOutput, calls=%fused_computation.104 | convolution fusion | flops 134216704 | bytes 25300996 | tf_op jit(solution)/shard_map/dot_general | solution.py:45
  105.5 10.7 %all-reduce.20.cloned.1.call-start = ((), (), s32[]{:S(2)}) async-start(), calls=%async_computation.2 | async-start | bytes 262144 | tf_op jit(solution)/shard_map/psum | solution.py:78
  118.6 7.4 fusion.13
  126.0 13.1 %all-reduce.8 = (f32[10,1024]{1,0:T(8,128)S(1)}, f32[1024]{0:T(1024)S(1)}) all-reduce(f32[10,1024]{1,0:T(8,128)S(1)} %fusion.13, f32[1024]{0:T(1024)S(1)} %convert_element_type.11), channel_id=1, replica_groups=mesh['samp'=32,'var'=4] {'var'}, use_global_device_ids=true, to_apply=%region_1.0 | all-reduce | flops 11264 | bytes 90112 | tf_op jit(solution)/shard_map/psum | solution.py:76
  139.2 65.9 %all-reduce.22.cloned.1.call-done = (f32[10,1024]{1,0:T(8,128)}, f32[10,1024]{1,0:T(8,128)}) async-done(((f32[10,1024]{1,0:T(8,128)}, f32[10,1024]{1,0:T(8,128)}), (f32[10,1024]{1,0:T(8,128)}, f32[10,1024]{1,0:T(8,128)})) %all-reduce.22.cloned.1.call-update) | async-done | bytes 81936 | tf_op jit(solution)/shard_map/psum | solution.py:78
  206.6 9.0 fusion.77
  225.4 14.0 %psum.194 = f32[10,1024]{1,0:T(8,128)S(1)} all-reduce(f32[10,1024]{1,0:T(8,128)S(1)} %fusion.16), channel_id=1, replica_groups=mesh['samp'=32,'var'=4] {'var'}, use_global_device_ids=true, to_apply=%region_9.10 | all-reduce | flops 10240 | bytes 81920 | tf_op jit(solution)/shard_map/psum | solution.py:76
  240.0 125.1 %all-reduce.23 = (f32[10,1024]{1,0:T(8,128)S(1)}, f32[10,1024]{1,0:T(8,128)S(1)}, f32[]{:T(128)}, f32[]{:T(128)}) all-reduce(f32[10,1024]{1,0:T(8,128)S(1)} %fusion.80, f32[10,1024]{1,0:T(8,128)S(1)} %fusion.65, f32[]{:T(128)} %get-tuple-element.5, f32[]{:T(128)} %get-tuple-element.4), channel_id=1, replica_groups=mesh['samp'=32,'var'=4] {'samp'}, use_global_device_ids=true, to_apply=%region_16.17 | all-reduce | flops 20482 | bytes 163856 | tf_op jit(solution)/shard_map/psum | solution.py:78
  375.5 9.0 fusion.73
  392.9 7.3 fusion.19
  400.3 12.7 %psum.200 = f32[10,1024]{1,0:T(8,128)S(1)} all-reduce(f32[10,1024]{1,0:T(8,128)S(1)} %fusion.19), channel_id=1, replica_groups=mesh['samp'=32,'var'=4] {'var'}, use_global_device_ids=true, to_apply=%region_20.21 | all-reduce | flops 10240 | bytes 81920 | tf_op jit(solution)/shard_map/psum | solution.py:76
  413.3 106.5 %all-reduce.20.cloned.1.call-done = (f32[10,1024]{1,0:T(8,128)}, f32[10,1024]{1,0:T(8,128)}) async-done(((f32[10,1024]{1,0:T(8,128)}, f32[10,1024]{1,0:T(8,128)}), (f32[10,1024]{1,0:T(8,128)}, f32[10,1024]{1,0:T(8,128)})) %all-reduce.20.cloned.1.call-update) | async-done | bytes 81936 | tf_op jit(solution)/shard_map/psum | solution.py:78
  520.7 9.0 fusion.72
  538.1 7.3 fusion.22
  545.4 13.9 %psum.203 = f32[10,1024]{1,0:T(8,128)S(1)} all-reduce(f32[10,1024]{1,0:T(8,128)S(1)} %fusion.22), channel_id=1, replica_groups=mesh['samp'=32,'var'=4] {'var'}, use_global_device_ids=true, to_apply=%region_24.25 | all-reduce | flops 10240 | bytes 81920 | tf_op jit(solution)/shard_map/psum | solution.py:76
  559.7 102.3 %all-reduce.18.cloned.1.call-done = (f32[10,1024]{1,0:T(8,128)}, f32[10,1024]{1,0:T(8,128)}) async-done(((f32[10,1024]{1,0:T(8,128)}, f32[10,1024]{1,0:T(8,128)}), (f32[10,1024]{1,0:T(8,128)}, f32[10,1024]{1,0:T(8,128)})) %all-reduce.18.cloned.1.call-update) | async-done | bytes 81936 | tf_op jit(solution)/shard_map/psum | solution.py:78
  663.0 9.0 fusion.71
  681.7 13.9 %psum.207 = f32[10,1024]{1,0:T(8,128)S(1)} all-reduce(f32[10,1024]{1,0:T(8,128)S(1)} %fusion.25), channel_id=1, replica_groups=mesh['samp'=32,'var'=4] {'var'}, use_global_device_ids=true, to_apply=%region_30.31 | all-reduce | flops 10240 | bytes 81920 | tf_op jit(solution)/shard_map/psum | solution.py:76
  696.3 125.1 %all-reduce.24 = (f32[10,1024]{1,0:T(8,128)S(1)}, f32[10,1024]{1,0:T(8,128)S(1)}, f32[]{:T(128)}, f32[]{:T(128)}) all-reduce(f32[10,1024]{1,0:T(8,128)S(1)} %fusion.82, f32[10,1024]{1,0:T(8,128)S(1)} %fusion.57, f32[]{:T(128)} %get-tuple-element.3, f32[]{:T(128)} %get-tuple-element.2), channel_id=1, replica_groups=mesh['samp'=32,'var'=4] {'samp'}, use_global_device_ids=true, to_apply=%region_37.38 | all-reduce | flops 20482 | bytes 163856 | tf_op jit(solution)/shard_map/psum | solution.py:78
  832.3 9.0 fusion.68
  849.8 7.3 fusion.28
  857.1 12.7 %psum.213 = f32[10,1024]{1,0:T(8,128)S(1)} all-reduce(f32[10,1024]{1,0:T(8,128)S(1)} %fusion.28), channel_id=1, replica_groups=mesh['samp'=32,'var'=4] {'var'}, use_global_device_ids=true, to_apply=%region_41.42 | all-reduce | flops 10240 | bytes 81920 | tf_op jit(solution)/shard_map/psum | solution.py:76
  870.5 106.0 %all-reduce.16.cloned.1.call-done = (f32[10,1024]{1,0:T(8,128)}, f32[10,1024]{1,0:T(8,128)}) async-done(((f32[10,1024]{1,0:T(8,128)}, f32[10,1024]{1,0:T(8,128)}), (f32[10,1024]{1,0:T(8,128)}, f32[10,1024]{1,0:T(8,128)})) %all-reduce.16.cloned.1.call-update) | async-done | bytes 81936 | tf_op jit(solution)/shard_map/psum | solution.py:78
  (76 shorter events, 92.7 us)
Async XLA Ops:
  7.2 197.9 %all-reduce.22.cloned.1.call-start = ((), (), s32[]{:S(2)}) async-start(), calls=%async_computation.3 | async-start | bytes 262144 | tf_op jit(solution)/shard_map/psum | solution.py:78
  77.2 5.4 copy-start.11
  94.6 2.0 copy-start
  94.6 6.2 copy-start.4
  94.6 6.2 copy-start.10
  105.5 414.3 %all-reduce.20.cloned.1.call-start = ((), (), s32[]{:S(2)}) async-start(), calls=%async_computation.2 | async-start | bytes 262144 | tf_op jit(solution)/shard_map/psum | solution.py:78
  206.6 9.0 copy-start.5
  375.5 9.1 copy-start.6
  384.5 4.2 copy-start.13
  384.5 4.2 copy-start.2
  413.0 249.0 %all-reduce.18.cloned.1.call-start = ((), (), s32[]{:S(2)}) async-start(), calls=%async_computation.1 | async-start | bytes 262144 | tf_op jit(solution)/shard_map/psum | solution.py:78
  520.7 9.1 copy-start.7
  529.7 4.2 copy-start.14
  529.7 4.2 copy-start.3
  559.4 417.1 %all-reduce.16.cloned.1.call-start = ((), (), s32[]{:S(2)}) async-start(), calls=%async_computation | async-start | bytes 262144 | tf_op jit(solution)/shard_map/psum | solution.py:78
  663.0 9.0 copy-start.8
  832.3 9.1 copy-start.9
  841.4 4.2 copy-start.12
  841.4 4.2 copy-start.1
Sparse Core Ops, SparseCore 0:
  105.6 99.4 all-reduce.21
  413.2 106.5 all-reduce.19
  559.5 102.4 all-reduce.17
  870.0 106.4 all-reduce.15
where the time goes:
time: 994 us; the launch traced here: 985 us
  blocking collectives  409 us (41%)
  waiting for transfers between devices  381 us (38%)
  matrix products  140 us (14%)
  between operations  19.9 us (2%)
  local copies, waits for them, and re-layouts  13.3 us (1%)
  other arithmetic  11.3 us (1%)
  starting transfers between devices  11.2 us (1%)
    psum x4, waiting for transfers between devices, expectation_step(): alt_sums, ref_sums = lax.psum((alt_terms, ref_terms), 'samp')  381 us
    psum x2, blocking collectives, expectation_step(): alt_sums, ref_sums = lax.psum((alt_terms, ref_terms), 'samp')  250 us
    psum x6, blocking collectives, expectation_step(): prop_sums = lax.psum(prop_terms, 'var')  80.4 us
    all_gather x1, blocking collectives, local(): gathered = lax.all_gather(frequencies, ('samp', 'var'), axis=1, tiled=True)  64.1 us
    dot_general x6, matrix products, expectation_step(): lax.dot_general(mixture, current, (((0,), (0,)), ((), ())), precision=EXA...  57.1 us
    dot_general x6, matrix products, expectation_step(): lax.dot_general(current, ratio_alt - ratio_ref, (((1,), (1,)), ((), ())),...  34.7 us
    dot_general x6, matrix products, expectation_step(): lax.dot_general(mixture, ratio_alt, (((1,), (0,)), ((), ())), precision=E...  24.2 us
    dot_general x6, matrix products, expectation_step(): lax.dot_general(mixture, ratio_ref, (((1,), (0,)), ((), ())), precision=E...  24 us
  transfers between devices with their start and end apart: 4, of which 4 were waited for; matrix products, arithmetic and copies ran while one was open for 1% of the time, Pallas kernels for 0%

commit v1 on v0

--- a/solution.py
+++ b/solution.py
@@ -73,7 +73,10 @@
             precision=EXACT,
             preferred_element_type=jnp.float32,
         )
-        prop_sums = lax.psum(prop_terms, "var")
+        ndev = lax.axis_size("var")
+        prop_sums = prop_terms
+        for jj in [[(rr, rr ^ m) for rr in range(ndev)] for m in (1, 2, 4, 8, 16) if m < ndev]:
+            prop_sums = prop_sums + lax.ppermute(prop_sums, "var", jj)
         next_mixture = clip_unit(mixture * prop_sums / twice_observed)
         alt_sums, ref_sums = lax.psum((alt_terms, ref_terms), "samp")
         next_alleles = allele_rule(current, alt_sums, ref_sums)

time: 994 us -> 917 us (0.923)
  blocking collectives: 409 us -> 335 us
  matrix products: 140 us -> 121 us
  waiting for transfers between devices: 381 us -> 391 us
    psum x6 -> x1, blocking collectives: 80.4 us -> 7.45 us  [local(): twice_observed = 2.0 * lax.psum(local_counts, 'var')[None, :]]
    dot_general x6, matrix products: 34.7 us -> 16 us  [expectation_step(): lax.dot_general(current, ratio_alt - ratio_ref, (((1,), (1,)), ((), ())),...]
    ppermute x0 -> x12, starting transfers between devices: none -> 18.4 us  [expectation_step(): prop_sums = prop_sums + lax.ppermute(prop_sums, 'var', jj)]
    psum x4, starting transfers between devices: 11.2 us -> 0.16 us  [expectation_step(): alt_sums, ref_sums = lax.psum((alt_terms, ref_terms), 'samp')]
    psum x4, waiting for transfers between devices: 381 us -> 391 us  [expectation_step(): alt_sums, ref_sums = lax.psum((alt_terms, ref_terms), 'samp')]
  transfers between devices with their start and end apart: 4 -> 16, of which waited for: 4 -> 4; matrix products, arithmetic and copies ran while one was open for 1% -> 5% of each run, Pallas kernels for 0% -> 0%
where the time goes in v1:
time: 917 us; the launch traced here: 910 us
  waiting for transfers between devices  391 us (43%)
  blocking collectives  335 us (37%)
  matrix products  121 us (13%)
  between operations  19.7 us (2%)
  starting transfers between devices  18.5 us (2%)
  other arithmetic  12.6 us (1%)
  local copies, waits for them, and re-layouts  11.3 us (1%)
    psum x4, waiting for transfers between devices, expectation_step(): alt_sums, ref_sums = lax.psum((alt_terms, ref_terms), 'samp')  391 us
    psum x2, blocking collectives, expectation_step(): alt_sums, ref_sums = lax.psum((alt_terms, ref_terms), 'samp')  249 us
    all_gather x1, blocking collectives, local(): gathered = lax.all_gather(frequencies, ('samp', 'var'), axis=1, tiled=True)  64.1 us
    dot_general x6, matrix products, expectation_step(): lax.dot_general(mixture, current, (((0,), (0,)), ((), ())), precision=EXA...  57.1 us
    dot_general x6, matrix products, expectation_step(): lax.dot_general(mixture, ratio_alt, (((1,), (0,)), ((), ())), precision=E...  24.2 us
    dot_general x6, matrix products, expectation_step(): lax.dot_general(mixture, ratio_ref, (((1,), (0,)), ((), ())), precision=E...  23.8 us
    ppermute x12, starting transfers between devices, expectation_step(): prop_sums = prop_sums + lax.ppermute(prop_sums, 'var', jj)  18.4 us
  transfers between devices with their start and end apart: 16, of which 4 were waited for; matrix products, arithmetic and copies ran while one was open for 5% of the time, Pallas kernels for 0%

profile of v1, /device:TPU:1, one launch (start us, length us, event | category | flops | bytes accessed | tf_op | source)
XLA Modules:
  0.0 909.6 jit_solution(1540331181360101507)
XLA Ops:
  7.2 64.1 %all-gather = f32[128,32,10]{1,2,0:T(8,128)S(1)} all-gather(f32[1,32,10]{1,2,0:T(8,128)} %bitcast.70), channel_id=1, replica_groups=mesh['samp'=32,'var'=4] {'samp','var'}, dimensions={0}, use_global_device_ids=true | all-gather | bytes 165120 | tf_op jit(solution)/shard_map/all_gather | solution.py:32
  71.8 5.3 copy.14
  77.2 5.4 copy.13
  82.6 12.0 %fusion.78 = (f32[1024]{0:T(1024)S(1)}, f32[1024,1024]{0,1:T(8,128)S(1)}, f32[1024,1024]{0,1:T(8,128)}, f32[1024,1024]{0,1:T(8,128)S(1)}, f32[1024,1024]{1,0:T(8,128)S(1)}) fusion(s32[1024,1024]{0,1:T(8,128)} %copy.14, s32[1024,1024]{0,1:T(8,128)} %copy.13, f32[10,1024]{1,0:T(8,128)S(1)} %copy-done.6, f32[4096,10]{0,1:T(8,128)S(1)} %reshape.15, ...), kind=kOutput, calls=%fused_computation.104 | convolution fusion | flops 134216704 | bytes 25300996 | tf_op jit(solution)/shard_map/dot_general | solution.py:45
  97.7 4.7 convolution_bitcast_fusion.1
  102.4 4.3 convolution_bitcast_fusion
  109.2 7.4 psum.147
  117.3 90.2 %all-reduce.21.cloned.1.call-done = (f32[10,1024]{1,0:T(8,128)}, f32[10,1024]{1,0:T(8,128)}) async-done(((f32[10,1024]{1,0:T(8,128)}, f32[10,1024]{1,0:T(8,128)}), (f32[10,1024]{1,0:T(8,128)}, f32[10,1024]{1,0:T(8,128)})) %all-reduce.21.cloned.1.call-update) | async-done | bytes 81936 | tf_op jit(solution)/shard_map/psum | solution.py:81
  209.1 9.0 fusion.77
  233.2 124.6 %all-reduce.22 = (f32[10,1024]{1,0:T(8,128)S(1)}, f32[10,1024]{1,0:T(8,128)S(1)}, f32[]{:T(128)}, f32[]{:T(128)}) all-reduce(f32[10,1024]{1,0:T(8,128)S(1)} %fusion.80, f32[10,1024]{1,0:T(8,128)S(1)} %fusion.65, f32[]{:T(128)} %multiply_reduce_fusion.7, f32[]{:T(128)} %get-tuple-element.44), channel_id=1, replica_groups=mesh['samp'=32,'var'=4] {'samp'}, use_global_device_ids=true, to_apply=%region_14.15 | all-reduce | flops 20482 | bytes 163856 | tf_op jit(solution)/shard_map/psum | solution.py:81
  359.7 7.2 all-reduce.7
  368.4 9.0 fusion.73
  377.4 4.2 fusion.50
  391.2 101.5 %all-reduce.19.cloned.1.call-done = (f32[10,1024]{1,0:T(8,128)}, f32[10,1024]{1,0:T(8,128)}) async-done(((f32[10,1024]{1,0:T(8,128)}, f32[10,1024]{1,0:T(8,128)}), (f32[10,1024]{1,0:T(8,128)}, f32[10,1024]{1,0:T(8,128)})) %all-reduce.19.cloned.1.call-update) | async-done | bytes 81936 | tf_op jit(solution)/shard_map/psum | solution.py:81
  493.7 9.0 fusion.72
  502.8 4.2 fusion.60
  510.9 4.2 fusion.81
  518.0 97.6 %all-reduce.17.cloned.1.call-done = (f32[10,1024]{1,0:T(8,128)}, f32[10,1024]{1,0:T(8,128)}) async-done(((f32[10,1024]{1,0:T(8,128)}, f32[10,1024]{1,0:T(8,128)}), (f32[10,1024]{1,0:T(8,128)}, f32[10,1024]{1,0:T(8,128)})) %all-reduce.17.cloned.1.call-update) | async-done | bytes 81936 | tf_op jit(solution)/shard_map/psum | solution.py:81
  616.5 9.0 fusion.71
  640.5 124.7 %all-reduce.23 = (f32[10,1024]{1,0:T(8,128)S(1)}, f32[10,1024]{1,0:T(8,128)S(1)}, f32[]{:T(128)}, f32[]{:T(128)}) all-reduce(f32[10,1024]{1,0:T(8,128)S(1)} %fusion.82, f32[10,1024]{1,0:T(8,128)S(1)} %fusion.57, f32[]{:T(128)} %multiply_reduce_fusion.3, f32[]{:T(128)} %get-tuple-element.29), channel_id=1, replica_groups=mesh['samp'=32,'var'=4] {'samp'}, use_global_device_ids=true, to_apply=%region_32.33 | all-reduce | flops 20482 | bytes 163856 | tf_op jit(solution)/shard_map/psum | solution.py:81
  767.7 7.2 all-reduce.6
  776.4 9.0 fusion.68
  785.4 4.2 fusion.53
  798.8 101.9 %all-reduce.15.cloned.1.call-done = (f32[10,1024]{1,0:T(8,128)}, f32[10,1024]{1,0:T(8,128)}) async-done(((f32[10,1024]{1,0:T(8,128)}, f32[10,1024]{1,0:T(8,128)}), (f32[10,1024]{1,0:T(8,128)}, f32[10,1024]{1,0:T(8,128)})) %all-reduce.15.cloned.1.call-update) | async-done | bytes 81936 | tf_op jit(solution)/shard_map/psum | solution.py:81
  (87 shorter events, 70.2 us)
Async XLA Ops:
  7.2 200.4 %all-reduce.21.cloned.1.call-start = ((), (), s32[]{:S(2)}) async-start(), calls=%async_computation.3 | async-start | bytes 262144 | tf_op jit(solution)/shard_map/psum | solution.py:81
  77.2 5.4 copy-start.6
  94.6 3.1 copy-start
  97.2 19.4 %collective-permute-start = (f32[10,1024]{1,0:T(8,128)S(1)}, f32[10,1024]{1,0:T(8,128)S(1)}, u32[]{:S(2)}, u32[]{:S(2)}) collective-permute-start(f32[10,1024]{1,0:T(8,128)S(1)} %fusion.13), channel_id=1, source_target_pairs={{0,1},{1,0},{2,3},{3,2},{4,5},{5,4},{6,7},{7,6},{8,9},{9,8},{10,11... | collective-permute-start | bytes 122888 | tf_op jit(solution)/shard_map/ppermute | solution.py:79
  106.6 386.1 %all-reduce.19.cloned.1.call-start = ((), (), s32[]{:S(2)}) async-start(), calls=%async_computation.2 | async-start | bytes 262144 | tf_op jit(solution)/shard_map/psum | solution.py:81
  116.6 92.4 %collective-permute-start.1 = (f32[10,1024]{1,0:T(8,128)S(1)}, f32[10,1024]{1,0:T(8,128)S(1)}, u32[]{:S(2)}, u32[]{:S(2)}) collective-permute-start(f32[10,1024]{1,0:T(8,128)S(1)} %add.186), channel_id=1, source_target_pairs={{0,2},{1,3},{2,0},{3,1},{4,6},{5,7},{6,4},{7,5},{8,10},{9,11},{10,... | collective-permute-start | bytes 122888 | tf_op jit(solution)/shard_map/ppermute | solution.py:79
  209.1 9.0 copy-start.1
  220.8 5.0 collective-permute-start.2
  225.8 6.2 collective-permute-start.3
  368.3 9.0 copy-start.2
  384.2 5.3 collective-permute-start.4
  389.5 226.0 %all-reduce.17.cloned.1.call-start = ((), (), s32[]{:S(2)}) async-start(), calls=%async_computation.1 | async-start | bytes 262144 | tf_op jit(solution)/shard_map/psum | solution.py:81
  389.6 104.1 %collective-permute-start.5 = (f32[10,1024]{1,0:T(8,128)S(1)}, f32[10,1024]{1,0:T(8,128)S(1)}, u32[]{:S(2)}, u32[]{:S(2)}) collective-permute-start(f32[10,1024]{1,0:T(8,128)S(1)} %add.202), channel_id=1, source_target_pairs={{0,2},{1,3},{2,0},{3,1},{4,6},{5,7},{6,4},{7,5},{8,10},{9,11},{10,... | collective-permute-start | bytes 122888 | tf_op jit(solution)/shard_map/ppermute | solution.py:79
  493.7 9.0 copy-start.3
  509.6 5.5 collective-permute-start.6
  515.1 385.6 %all-reduce.15.cloned.1.call-start = ((), (), s32[]{:S(2)}) async-start(), calls=%async_computation | async-start | bytes 262144 | tf_op jit(solution)/shard_map/psum | solution.py:81
  515.2 101.3 %collective-permute-start.7 = (f32[10,1024]{1,0:T(8,128)S(1)}, f32[10,1024]{1,0:T(8,128)S(1)}, u32[]{:S(2)}, u32[]{:S(2)}) collective-permute-start(f32[10,1024]{1,0:T(8,128)S(1)} %add.207), channel_id=1, source_target_pairs={{0,2},{1,3},{2,0},{3,1},{4,6},{5,7},{6,4},{7,5},{8,10},{9,11},{10,... | collective-permute-start | bytes 122888 | tf_op jit(solution)/shard_map/ppermute | solution.py:79
  616.5 9.0 copy-start.4
  628.2 4.8 collective-permute-start.8
  633.0 6.2 collective-permute-start.9
  776.3 9.0 copy-start.5
  792.2 5.3 collective-permute-start.10
  797.5 104.7 %collective-permute-start.11 = (f32[10,1024]{1,0:T(8,128)S(1)}, f32[10,1024]{1,0:T(8,128)S(1)}, u32[]{:S(2)}, u32[]{:S(2)}) collective-permute-start(f32[10,1024]{1,0:T(8,128)S(1)} %add.223), channel_id=1, source_target_pairs={{0,2},{1,3},{2,0},{3,1},{4,6},{5,7},{6,4},{7,5},{8,10},{9,11},{10,... | collective-permute-start | bytes 122888 | tf_op jit(solution)/shard_map/ppermute | solution.py:79
Sparse Core Ops, SparseCore 0:
  106.8 100.7 all-reduce.20
  389.6 103.1 all-reduce.18
  515.2 100.2 all-reduce.16
  797.6 103.0 all-reduce.14
